TPU v7x, 32 devices: a whole 2x2x4 slice. The times are simulated.
32 devices in a mesh: seq: 4 (over y, core), dp: 8 (over z, x).
Axes of the slice: x: 2, y: 2, z: 4, core: 2. Of those that a mesh axis runs over, the one named last changes fastest.
Arguments:
- mlp_hidden: bfloat16 [8, 256, 8192], P('dp', None, 'seq'), may hold values from -6 to 6
- encoder_stream: bfloat16 [8, 256, 4096], P('dp', 'seq'), may hold values from -18 to 18
- down_proj: bfloat16 [8192, 4096], P('seq', 'dp'), may hold values from -0.0625 to 0.0625
- final_gain: bfloat16 [4096], replicated, may hold values from 0.25 to 1.75
- kv_proj: bfloat16 [4096, 2, 2048], P('dp', None, 'seq'), may hold values from -0.09375 to 0.09375
- queries: bfloat16 [8, 128, 2048], P('dp', None, 'seq'), may hold values from -640 to 640
- out_proj: bfloat16 [2048, 4096], P('seq'), may hold values from -0.39648438 to 0.39648438
- enc_len: int32 [8], P('dp'), may hold values from 128 to 256, as said below
- dec_pad: int32 [8], P('dp'), may hold values from 0 to 64, as said below
Outputs:
- cross_out: bfloat16 [8, 128, 4096], P('dp', 'seq')
Inputs may be any that keep to these rules, and one draw needn't show every extreme that they name: `enc_len`: at least one filing uses all 256 positions and one uses 256 // 2. `dec_pad`: some filing has no padding and some has 64 padded rows.
All inputs are finite; a program needn't handle non-finite values.
Results may differ from a plain program's by a relative error of at most 0.015.
The roundings to bfloat16 on the way count: a program that leaves them out, or rounds other values in their place, can miss the bound.
Values may be sent and summed in bfloat16 or wider, within the bound.
No kernel may reach another device: no remote copies, remote signals or barrier semaphores. Data moves between devices by JAX's collectives and lax.ppermute only.
A program may use at most 128 MiB of HBM per device.

v0:
```python
import math
import jax
import jax.numpy as jnp
from jax import lax
from jax.sharding import PartitionSpec as P

HD = 256


def normalize(resid, gain_row):
    spread = jnp.mean(resid * resid, axis=-1, keepdims=True)
    return (resid * lax.rsqrt(spread + 1e-06) * gain_row).astype(jnp.bfloat16)


def on_device(
    mlp_hidden, encoder_stream, down_proj, final_gain, kv_proj, queries, out_proj, enc_len, dec_pad
):
    hidden = mlp_hidden[0]
    enc_total = hidden.shape[0]
    gain_row = final_gain.astype(jnp.float32)
    full_down = lax.all_gather(down_proj, "dp", axis=1, tiled=True)
    row_block = hidden
    mlp_out = lax.psum_scatter(
        jnp.dot(row_block, full_down, preferred_element_type=jnp.float32),
        "seq",
        scatter_dimension=0,
        tiled=True,
    )
    normed = normalize(encoder_stream[0].astype(jnp.float32) + mlp_out, gain_row)
    encoded = lax.all_gather(normed, "seq", axis=0, tiled=True)
    heads_here = queries.shape[2] // HD
    kv_width = 2 * heads_here * HD
    weight_piece = lax.all_gather(kv_proj, "dp", axis=0, tiled=True)
    key_value = jnp.dot(
        encoded,
        weight_piece.reshape(weight_piece.shape[0], kv_width),
        preferred_element_type=jnp.float32,
    ).astype(jnp.bfloat16)
    key_value = key_value.reshape(enc_total, 2, heads_here, HD)
    key_rows = key_value[:, 0]
    value_rows = key_value[:, 1]
    dec_rows = queries.shape[1]
    query_rows = queries[0].reshape(dec_rows, heads_here, HD)
    scores = jnp.einsum(
        "qhd,khd->hqk", query_rows, key_rows, preferred_element_type=jnp.float32
    ) / math.sqrt(HD)
    visible = jnp.arange(enc_total, dtype=jnp.int32) < enc_len[0]
    scores = jnp.where(visible[None, None, :], scores, -jnp.inf)
    highest = jnp.max(scores, axis=-1, keepdims=True)
    expo = jnp.exp(scores - highest)
    attention = (expo / jnp.sum(expo, axis=-1, keepdims=True)).astype(jnp.bfloat16)
    attended = jnp.einsum(
        "hqk,khd->qhd", attention, value_rows, preferred_element_type=jnp.float32
    ).astype(jnp.bfloat16)
    row_live = jnp.arange(dec_rows, dtype=jnp.int32) < dec_rows - dec_pad[0]
    attended = jnp.where(row_live[:, None, None], attended, jnp.zeros_like(attended)).reshape(
        dec_rows, heads_here * HD
    )
    row_block = attended
    result = lax.psum_scatter(
        jnp.dot(row_block, out_proj, preferred_element_type=jnp.float32),
        "seq",
        scatter_dimension=0,
        tiled=True,
    )
    return result.astype(jnp.bfloat16)[None]


def solution(mesh):
    placed = (
        P("dp", None, "seq"),
        P("dp", "seq", None),
        P("seq", "dp"),
        P(),
        P("dp", None, "seq"),
        P("dp", None, "seq"),
        P("seq", None),
        P("dp"),
        P("dp"),
    )
    return jax.shard_map(
        on_device, mesh=mesh, in_specs=placed, out_specs=P("dp", "seq", None), check_vma=False
    )
```

profile of v0, /device:TPU:0, one launch (start us, length us, event | category | flops | bytes accessed | tf_op | source)
XLA Modules:
  0.0 494.5 jit_solution(16718448679306863005)
XLA Ops:
  6.5 0.0 copy-start
  6.5 0.0 all-gather.4.cloned.1.call-start
  6.5 0.7 all-gather.4.cloned.1.call-update
  7.3 0.0 reduce-scatter.3.cloned.1.call-start
  7.3 232.6 %all-gather.4.cloned.1.call-done = bf16[2048,4096]{1,0:T(8,128)(2,1)} async-done(((bf16[2048,512]{1,0:T(8,128)(2,1)}), bf16[2048,4096]{1,0:T(8,128)(2,1)}) %all-gather.4.cloned.1.call-update) | async-done | bytes 16777232 | tf_op jit(solution)/shard_map/all_gather | solution.py:21
  239.9 0.0 copy-done
  239.9 10.1 %fusion.6 = f32[256,4096]{1,0:T(8,128)} fusion(bf16[2048,4096]{1,0:T(8,128)(2,1)} %all-gather.4.cloned.1.call-done, bf16[1,256,2048]{2,1,0:T(8,128)(2,1)S(1)} %copy-done), kind=kOutput, calls=%fused_computation.10 | convolution fusion | flops 4294967296 | bytes 22020096 | tf_op jit(solution)/shard_map/dot_general | solution.py:24
  250.0 0.0 copy-start.3
  250.0 0.0 copy-start.1
  250.0 0.0 copy-start.2
  250.0 0.0 reduce-scatter.3.cloned.1.call-update
  250.0 0.0 all-gather.8.cloned.1.call-start
  250.0 0.7 all-gather.8.cloned.1.call-update
  250.7 0.0 all-gather.6.cloned.1.call-start
  250.8 0.0 copy-done.3
  250.8 42.0 %reduce-scatter.3.cloned.1.call-done = f32[64,4096]{1,0:T(8,128)} async-done(((f32[256,4096]{1,0:T(8,128)}), f32[64,4096]{1,0:T(8,128)}) %reduce-scatter.3.cloned.1.call-update) | async-done | bytes 1048592 | tf_op jit(solution)/shard_map/reduce_scatter | solution.py:23
  292.8 0.0 copy-done.1
  292.8 1.5 multiply_reduce_fusion
  294.3 2.2 multiply_convert_fusion
  296.5 0.0 all-gather.6.cloned.1.call-update
  296.5 0.0 reduce-scatter.5.cloned.1.call-start
  296.6 0.0 copy-done.2
  297.9 122.2 %all-gather.8.cloned.1.call-done = bf16[4096,2,512]{2,1,0:T(2,128)(2,1)} async-done(((bf16[512,2,512]{2,1,0:T(2,128)(2,1)}), bf16[4096,2,512]{2,1,0:T(2,128)(2,1)}) %all-gather.8.cloned.1.call-update) | async-done | bytes 8388624 | tf_op jit(solution)/shard_map/all_gather | solution.py:33
  420.1 9.3 %copy.21 = bf16[512,8,2,512]{3,1,2,0:T(8,128)(2,1)} copy(bf16[512,8,2,512]{3,2,1,0:T(2,128)(2,1)} %bitcast.32) | data formatting | bytes 16777216
  429.4 13.0 %all-gather.6.cloned.1.call-done = bf16[256,4096]{1,0:T(8,128)(2,1)} async-done(((bf16[64,4096]{1,0:T(8,128)(2,1)}), bf16[256,4096]{1,0:T(8,128)(2,1)}) %all-gather.6.cloned.1.call-update) | async-done | bytes 2097168 | tf_op jit(solution)/shard_map/all_gather | solution.py:30
  442.4 6.3 %convolution_convert_fusion = bf16[256,1024]{1,0:T(8,128)(2,1)S(1)} fusion(bf16[256,4096]{1,0:T(8,128)(2,1)} %all-gather.6.cloned.1.call-done, bf16[4096,1024]{1,0:T(8,128)(2,1)} %bitcast.33), kind=kOutput, calls=%fused_computation.1 | convolution fusion | flops 2147745792 | bytes 11010048 | tf_op jit(solution)/shard_map/dot_general | solution.py:34
  448.8 0.4 reshape.33
  449.2 0.4 fusion.12
  449.5 0.2 fusion.3
  449.8 0.1 fusion.13
  449.9 0.2 copy.19
  450.1 0.3 fusion.5
  450.3 4.3 fusion.14
  454.6 0.0 reduce-scatter.5.cloned.1.call-update
  454.6 31.6 %reduce-scatter.5.cloned.1.call-done = f32[32,4096]{1,0:T(8,128)} async-done(((f32[128,4096]{1,0:T(8,128)}), f32[32,4096]{1,0:T(8,128)}) %reduce-scatter.5.cloned.1.call-update) | async-done | bytes 524304 | tf_op jit(solution)/shard_map/reduce_scatter | solution.py:60
  486.2 1.8 convert_bitcast_fusion
  (5 shorter events, 0.1 us)
Async XLA Ops:
  6.5 233.4 %copy-start = (bf16[1,256,2048]{2,1,0:T(8,128)(2,1)S(1)}, bf16[1,256,2048]{2,1,0:T(8,128)(2,1)}, u32[]{:S(2)}) copy-start(bf16[1,256,2048]{2,1,0:T(8,128)(2,1)} %param.9) | copy-start | bytes 3145732
  6.5 233.3 %all-gather.4.cloned.1.call-start = ((), (), s32[]{:S(2)}) async-start(), calls=%async_computation.2 | async-start | bytes 18874368 | tf_op jit(solution)/shard_map/all_gather | solution.py:21
  7.3 285.6 %reduce-scatter.3.cloned.1.call-start = ((), (), s32[]{:S(2)}) async-start(), calls=%async_computation.3 | async-start | bytes 5242880 | tf_op jit(solution)/shard_map/reduce_scatter | solution.py:23
  250.0 0.8 copy-start.3
  250.0 42.9 %copy-start.1 = (bf16[1,64,4096]{2,1,0:T(8,128)(2,1)S(1)}, bf16[1,64,4096]{2,1,0:T(8,128)(2,1)}, u32[]{:S(2)}) copy-start(bf16[1,64,4096]{2,1,0:T(8,128)(2,1)} %param.10) | copy-start | bytes 1572868
  250.0 46.6 %copy-start.2 = (bf16[1,128,512]{2,1,0:T(8,128)(2,1)S(1)}, bf16[1,128,512]{2,1,0:T(8,128)(2,1)}, u32[]{:S(2)}) copy-start(bf16[1,128,512]{2,1,0:T(8,128)(2,1)} %param.14) | copy-start | bytes 393220
  250.0 170.1 %all-gather.8.cloned.1.call-start = ((), (), s32[]{:S(2)}) async-start(), calls=%async_computation.5 | async-start | bytes 9437184 | tf_op jit(solution)/shard_map/all_gather | solution.py:33
  250.7 191.7 %all-gather.6.cloned.1.call-start = ((), (), s32[]{:S(2)}) async-start(), calls=%async_computation.4 | async-start | bytes 2621440 | tf_op jit(solution)/shard_map/all_gather | solution.py:30
  296.5 189.7 %reduce-scatter.5.cloned.1.call-start = ((), (), s32[]{:S(2)}) async-start(), calls=%async_computation.6 | async-start | bytes 2621440 | tf_op jit(solution)/shard_map/reduce_scatter | solution.py:60
Sparse Core Ops, SparseCore 0:
  9.4 230.4 all-gather.3
  250.1 42.6 reduce-scatter.2
  295.2 124.9 all-gather.7
  421.6 20.7 all-gather.5
  454.8 31.3 reduce-scatter.4
where the time goes:
time: 495 us
  waiting for transfers between devices  443 us (89%)
  matrix products  21.2 us (4%)
  between operations  14.5 us (3%)
  local copies, waits for them, and re-layouts  10.3 us (2%)
  other arithmetic  5.56 us (1%)
    all_gather x1, waiting for transfers between devices, on_device(): full_down = lax.all_gather(down_proj, 'dp', axis=1, tiled=True)  233 us
    all_gather x1, waiting for transfers between devices, on_device(): weight_piece = lax.all_gather(kv_proj, 'dp', axis=0, tiled=True)  122 us
    reduce_scatter x1, waiting for transfers between devices, on_device(): lax.psum_scatter(jnp.dot(row_block, full_down, preferred_element_type=jnp...  42 us
    reduce_scatter x1, waiting for transfers between devices, on_device(): lax.psum_scatter(jnp.dot(row_block, out_proj, preferred_element_type=jnp....  31.6 us
    all_gather x1, waiting for transfers between devices, on_device(): encoded = lax.all_gather(normed, 'seq', axis=0, tiled=True)  13 us
    dot_general x1, matrix products, on_device(): jnp.dot(row_block, full_down, preferred_element_type=jnp.float32)  10.1 us
  transfers between devices with their start and end apart: 5, of which 5 were waited for; matrix products, arithmetic and copies ran while one was open for 3% of the time, Pallas kernels for 0%

commit v1 on v0

--- a/solution.py
+++ b/solution.py
@@ -18,7 +18,14 @@
     hidden = mlp_hidden[0]
     enc_total = hidden.shape[0]
     gain_row = final_gain.astype(jnp.float32)
-    full_down = lax.all_gather(down_proj, "dp", axis=1, tiled=True)
+    ways = lax.axis_size("dp")
+    pieces = [down_proj]
+    for far in range(1, ways):
+        pieces.append(
+            lax.ppermute(pieces[far - 1], "dp", [(d, (d - 1) % ways) for d in range(ways)])
+        )
+    line = jnp.concatenate(pieces, axis=1)
+    full_down = jnp.roll(line, lax.axis_index("dp") * down_proj.shape[1], axis=1)
     row_block = hidden
     mlp_out = lax.psum_scatter(
         jnp.dot(row_block, full_down, preferred_element_type=jnp.float32),

time: 495 us -> 585 us (1.18)
  local copies, waits for them, and re-layouts: 10.3 us -> 57.7 us
  starting transfers between devices: 0.16 us -> 37.4 us
    ppermute x0 -> x7, waiting for transfers between devices: none -> 282 us  [on_device(): lax.ppermute(pieces[far - 1], 'dp', [(d, (d - 1) % ways) for d in range(w...]
    all_gather x1 -> x0, waiting for transfers between devices: 233 us -> none  [on_device(): full_down = lax.all_gather(down_proj, 'dp', axis=1, tiled=True)]
    all_gather x1, waiting for transfers between devices: 122 us -> 74.7 us  [on_device(): weight_piece = lax.all_gather(kv_proj, 'dp', axis=0, tiled=True)]
    unnamed x5, waiting for transfers between devices: 1.44 us -> 46 us
    reduce_scatter x1 -> x0, waiting for transfers between devices: 42 us -> none  [on_device(): lax.psum_scatter(jnp.dot(row_block, full_down, preferred_element_type=jnp...]
    unnamed x10 -> x48, local copies, waits for them, and re-layouts: 9.51 us -> 51.4 us
    ppermute x0 -> x7, starting transfers between devices: none -> 37 us  [on_device(): lax.ppermute(pieces[far - 1], 'dp', [(d, (d - 1) % ways) for d in range(w...]
  transfers between devices with their start and end apart: 5 -> 11, of which waited for: 5 -> 11; matrix products, arithmetic and copies ran while one was open for 3% -> 5% of each run, Pallas kernels for 0% -> 0%
where the time goes in v1:
time: 585 us; the launch traced here: 584 us
  waiting for transfers between devices  447 us (76%)
  local copies, waits for them, and re-layouts  57.7 us (10%)
  starting transfers between devices  37.4 us (6%)
  matrix products  21.6 us (4%)
  between operations  16.3 us (3%)
    ppermute x7, waiting for transfers between devices, on_device(): lax.ppermute(pieces[far - 1], 'dp', [(d, (d - 1) % ways) for d in range(w...  282 us
    all_gather x1, waiting for transfers between devices, on_device(): weight_piece = lax.all_gather(kv_proj, 'dp', axis=0, tiled=True)  74.7 us
    unnamed x48, local copies, waits for them, and re-layouts  51.4 us
    unnamed x5, waiting for transfers between devices  46 us
    ppermute x7, starting transfers between devices, on_device(): lax.ppermute(pieces[far - 1], 'dp', [(d, (d - 1) % ways) for d in range(w...  37 us
    reduce_scatter x1, waiting for transfers between devices, on_device(): lax.psum_scatter(jnp.dot(row_block, out_proj, preferred_element_type=jnp....  31.6 us
    all_gather x1, waiting for transfers between devices, on_device(): encoded = lax.all_gather(normed, 'seq', axis=0, tiled=True)  12.8 us
  transfers between devices with their start and end apart: 11, of which 11 were waited for; matrix products, arithmetic and copies ran while one was open for 5% of the time, Pallas kernels for 0%

profile of v1, /device:TPU:0, one launch (start us, length us, event | category | flops | bytes accessed | tf_op | source)
XLA Modules:
  0.0 584.1 jit_solution(14453828708154520900)
XLA Ops:
  7.4 6.0 %collective-permute-start = (bf16[2048,512]{1,0:T(8,128)(2,1)}, bf16[2048,512]{1,0:T(8,128)(2,1)S(1)}, u32[]{:S(2)}, u32[]{:S(2)}) collective-permute-start(bf16[2048,512]{1,0:T(8,128)(2,1)} %param.11), channel_id=1, source_target_pairs={{0,7},{1,0},{2,1},{3,2},{4,3},{5,4},{6,5},{7,6},{8,15},{9,8},{10,9... | collective-permute-start | bytes 6291464 | tf_op jit(solution)/shard_map/ppermute | solution.py:25
  13.3 45.2 %collective-permute-done = bf16[2048,512]{1,0:T(8,128)(2,1)S(1)} collective-permute-done((bf16[2048,512]{1,0:T(8,128)(2,1)}, bf16[2048,512]{1,0:T(8,128)(2,1)S(1)}, u32[]{:S(2)}, u32[]{:S(2)}) %collective-permute-start) | collective-permute-done | bytes 2097184 | tf_op jit(solution)/shard_map/ppermute | solution.py:25
  58.6 5.1 collective-permute-start.1
  63.6 44.0 %collective-permute-done.1 = bf16[2048,512]{1,0:T(8,128)(2,1)S(1)} collective-permute-done((bf16[2048,512]{1,0:T(8,128)(2,1)S(1)}, bf16[2048,512]{1,0:T(8,128)(2,1)S(1)}, u32[]{:S(2)}, u32[]{:S(2)}) %collective-permute-start.1) | collective-permute-done | bytes 2097184 | tf_op jit(solution)/shard_map/ppermute | solution.py:25
  107.6 1.3 copy-done.3
  109.0 5.2 collective-permute-start.2
  114.1 43.1 %collective-permute-done.2 = bf16[2048,512]{1,0:T(8,128)(2,1)S(1)} collective-permute-done((bf16[2048,512]{1,0:T(8,128)(2,1)S(1)}, bf16[2048,512]{1,0:T(8,128)(2,1)S(1)}, u32[]{:S(2)}, u32[]{:S(2)}) %collective-permute-start.2) | collective-permute-done | bytes 2097184 | tf_op jit(solution)/shard_map/ppermute | solution.py:25
  157.2 1.4 copy-done.5
  158.6 5.2 collective-permute-start.3
  163.8 42.2 %collective-permute-done.3 = bf16[2048,512]{1,0:T(8,128)(2,1)S(1)} collective-permute-done((bf16[2048,512]{1,0:T(8,128)(2,1)S(1)}, bf16[2048,512]{1,0:T(8,128)(2,1)S(1)}, u32[]{:S(2)}, u32[]{:S(2)}) %collective-permute-start.3) | collective-permute-done | bytes 2097184 | tf_op jit(solution)/shard_map/ppermute | solution.py:25
  206.0 1.3 copy-done.7
  207.3 5.2 collective-permute-start.4
  212.5 41.3 %collective-permute-done.4 = bf16[2048,512]{1,0:T(8,128)(2,1)S(1)} collective-permute-done((bf16[2048,512]{1,0:T(8,128)(2,1)S(1)}, bf16[2048,512]{1,0:T(8,128)(2,1)S(1)}, u32[]{:S(2)}, u32[]{:S(2)}) %collective-permute-start.4) | collective-permute-done | bytes 2097184 | tf_op jit(solution)/shard_map/ppermute | solution.py:25
  253.7 1.3 copy-done.9
  255.1 5.2 collective-permute-start.5
  260.2 40.3 %collective-permute-done.5 = bf16[2048,512]{1,0:T(8,128)(2,1)} collective-permute-done((bf16[2048,512]{1,0:T(8,128)(2,1)S(1)}, bf16[2048,512]{1,0:T(8,128)(2,1)}, u32[]{:S(2)}, u32[]{:S(2)}) %collective-permute-start.5) | collective-permute-done | bytes 2097184 | tf_op jit(solution)/shard_map/ppermute | solution.py:25
  300.6 5.3 collective-permute-start.6
  305.9 3.2 constant_dynamic-update-slice_fusion.15
  309.1 1.5 constant_dynamic-update-slice_fusion.14
  310.6 1.5 constant_dynamic-update-slice_fusion.13
  312.1 1.5 constant_dynamic-update-slice_fusion.12
  313.6 1.5 constant_dynamic-update-slice_fusion.11
  315.1 1.5 constant_dynamic-update-slice_fusion.10
  316.6 3.0 constant_dynamic-update-slice_fusion.9
  319.6 26.0 %collective-permute-done.6 = bf16[2048,512]{1,0:T(8,128)(2,1)} collective-permute-done((bf16[2048,512]{1,0:T(8,128)(2,1)}, bf16[2048,512]{1,0:T(8,128)(2,1)}, u32[]{:S(2)}, u32[]{:S(2)}) %collective-permute-start.6) | collective-permute-done | bytes 2097184 | tf_op jit(solution)/shard_map/ppermute | solution.py:25
  345.6 3.0 constant_dynamic-update-slice_fusion.8
  348.6 1.4 constant_dynamic-update-slice_fusion.7
  350.1 1.5 constant_dynamic-update-slice_fusion.6
  351.5 1.5 constant_dynamic-update-slice_fusion.5
  353.0 1.4 constant_dynamic-update-slice_fusion.4
  354.4 1.5 constant_dynamic-update-slice_fusion.3
  355.9 1.5 constant_dynamic-update-slice_fusion.2
  357.4 3.1 constant_dynamic-update-slice_fusion.1
  360.4 3.1 constant_dynamic-update-slice_fusion
  363.5 10.4 %fusion.3 = f32[256,4096]{0,1:T(8,128)} fusion(bf16[2048,8192]{1,0:T(8,128)(2,1)} %constant_dynamic-update-slice_fusion, s32[]{:T(128)S(6)} %select_n.28, bf16[1,256,2048]{2,1,0:T(8,128)(2,1)S(1)} %copy-done), kind=kOutput, calls=%fused_computation.3 | convolution fusion | flops 4294967296 | bytes 22020100 | tf_op jit(solution)/shard_map/dot_general | solution.py:31
  373.9 5.7 copy.22
  380.7 45.5 %reduce-scatter.7.cloned.1.call-done = f32[64,4096]{1,0:T(8,128)} async-done(((f32[256,4096]{1,0:T(8,128)}), f32[64,4096]{1,0:T(8,128)}) %reduce-scatter.7.cloned.1.call-update) | async-done | bytes 1048592
  426.2 1.8 copy.23
  428.0 0.6 multiply_reduce_fusion
  428.6 1.5 multiply_convert_fusion
  430.1 2.4 copy.16
  434.1 74.7 %all-gather.5.cloned.1.call-done = bf16[4096,2,512]{2,1,0:T(2,128)(2,1)} async-done(((bf16[512,2,512]{2,1,0:T(2,128)(2,1)}), bf16[4096,2,512]{2,1,0:T(2,128)(2,1)}) %all-gather.5.cloned.1.call-update) | async-done | bytes 8388624 | tf_op jit(solution)/shard_map/all_gather | solution.py:40
  508.8 9.3 %copy.26 = bf16[512,8,2,512]{3,1,2,0:T(8,128)(2,1)} copy(bf16[512,8,2,512]{3,2,1,0:T(2,128)(2,1)} %bitcast.34) | data formatting | bytes 16777216
  518.2 12.8 %all-gather.3.cloned.1.call-done = bf16[256,4096]{1,0:T(8,128)(2,1)} async-done(((bf16[64,4096]{1,0:T(8,128)(2,1)}), bf16[256,4096]{1,0:T(8,128)(2,1)}) %all-gather.3.cloned.1.call-update) | async-done | bytes 2097168 | tf_op jit(solution)/shard_map/all_gather | solution.py:37
  531.0 6.4 %convolution_convert_fusion = bf16[256,1024]{1,0:T(8,128)(2,1)S(1)} fusion(bf16[256,4096]{1,0:T(8,128)(2,1)} %all-gather.3.cloned.1.call-done, bf16[4096,1024]{1,0:T(8,128)(2,1)} %bitcast.35), kind=kOutput, calls=%fused_computation.7 | convolution fusion | flops 2147745792 | bytes 11010048 | tf_op jit(solution)/shard_map/dot_general | solution.py:41
  539.0 4.3 fusion.19
  543.3 31.6 %reduce-scatter.5.cloned.1.call-done = f32[32,4096]{1,0:T(8,128)} async-done(((f32[128,4096]{1,0:T(8,128)}), f32[32,4096]{1,0:T(8,128)}) %reduce-scatter.5.cloned.1.call-update) | async-done | bytes 524304 | tf_op jit(solution)/shard_map/reduce_scatter | solution.py:67
  574.9 1.8 convert_bitcast_fusion
  (44 shorter events, 3.0 us)
Async XLA Ops:
  7.4 356.1 %copy-start = (bf16[1,256,2048]{2,1,0:T(8,128)(2,1)S(1)}, bf16[1,256,2048]{2,1,0:T(8,128)(2,1)}, u32[]{:S(2)}) copy-start(bf16[1,256,2048]{2,1,0:T(8,128)(2,1)} %param.9) | copy-start | bytes 3145732
  7.4 418.8 %reduce-scatter.7.cloned.1.call-start = ((), (), s32[]{:S(2)}) async-start(), calls=%async_computation.5 | async-start | bytes 5242880
  7.4 51.2 %collective-permute-start = (bf16[2048,512]{1,0:T(8,128)(2,1)}, bf16[2048,512]{1,0:T(8,128)(2,1)S(1)}, u32[]{:S(2)}, u32[]{:S(2)}) collective-permute-start(bf16[2048,512]{1,0:T(8,128)(2,1)} %param.11), channel_id=1, source_target_pairs={{0,7},{1,0},{2,1},{3,2},{4,3},{5,4},{6,5},{7,6},{8,15},{9,8},{10,9... | collective-permute-start | bytes 6291464 | tf_op jit(solution)/shard_map/ppermute | solution.py:25
  58.6 49.1 %collective-permute-start.1 = (bf16[2048,512]{1,0:T(8,128)(2,1)S(1)}, bf16[2048,512]{1,0:T(8,128)(2,1)S(1)}, u32[]{:S(2)}, u32[]{:S(2)}) collective-permute-start(bf16[2048,512]{1,0:T(8,128)(2,1)S(1)} %collective-permute-done), channel_id=1, source_target_pairs={{0,7},{1,0},{2,1},{3,2},{4,3},{5,4},{6,5},{7,6},{8,15},{9,8},{10,9... | collective-permute-start | bytes 6291464 | tf_op jit(solution)/shard_map/ppermute | solution.py:25
  107.6 1.3 copy-start.3
  109.0 48.3 %collective-permute-start.2 = (bf16[2048,512]{1,0:T(8,128)(2,1)S(1)}, bf16[2048,512]{1,0:T(8,128)(2,1)S(1)}, u32[]{:S(2)}, u32[]{:S(2)}) collective-permute-start(bf16[2048,512]{1,0:T(8,128)(2,1)S(1)} %collective-permute-done.1), channel_id=1, source_target_pairs={{0,7},{1,0},{2,1},{3,2},{4,3},{5,4},{6,5},{7,6},{8,15},{9,8},{10,9... | collective-permute-start | bytes 6291464 | tf_op jit(solution)/shard_map/ppermute | solution.py:25
  157.2 1.4 copy-start.5
  158.6 47.4 %collective-permute-start.3 = (bf16[2048,512]{1,0:T(8,128)(2,1)S(1)}, bf16[2048,512]{1,0:T(8,128)(2,1)S(1)}, u32[]{:S(2)}, u32[]{:S(2)}) collective-permute-start(bf16[2048,512]{1,0:T(8,128)(2,1)S(1)} %collective-permute-done.2), channel_id=1, source_target_pairs={{0,7},{1,0},{2,1},{3,2},{4,3},{5,4},{6,5},{7,6},{8,15},{9,8},{10,9... | collective-permute-start | bytes 6291464 | tf_op jit(solution)/shard_map/ppermute | solution.py:25
  206.0 1.3 copy-start.7
  207.3 46.4 %collective-permute-start.4 = (bf16[2048,512]{1,0:T(8,128)(2,1)S(1)}, bf16[2048,512]{1,0:T(8,128)(2,1)S(1)}, u32[]{:S(2)}, u32[]{:S(2)}) collective-permute-start(bf16[2048,512]{1,0:T(8,128)(2,1)S(1)} %collective-permute-done.3), channel_id=1, source_target_pairs={{0,7},{1,0},{2,1},{3,2},{4,3},{5,4},{6,5},{7,6},{8,15},{9,8},{10,9... | collective-permute-start | bytes 6291464 | tf_op jit(solution)/shard_map/ppermute | solution.py:25
  253.7 1.3 copy-start.9
  255.1 45.5 %collective-permute-start.5 = (bf16[2048,512]{1,0:T(8,128)(2,1)S(1)}, bf16[2048,512]{1,0:T(8,128)(2,1)}, u32[]{:S(2)}, u32[]{:S(2)}) collective-permute-start(bf16[2048,512]{1,0:T(8,128)(2,1)S(1)} %collective-permute-done.4), channel_id=1, source_target_pairs={{0,7},{1,0},{2,1},{3,2},{4,3},{5,4},{6,5},{7,6},{8,15},{9,8},{10,9... | collective-permute-start | bytes 6291464 | tf_op jit(solution)/shard_map/ppermute | solution.py:25
  300.6 45.0 %collective-permute-start.6 = (bf16[2048,512]{1,0:T(8,128)(2,1)}, bf16[2048,512]{1,0:T(8,128)(2,1)}, u32[]{:S(2)}, u32[]{:S(2)}) collective-permute-start(bf16[2048,512]{1,0:T(8,128)(2,1)} %collective-permute-done.5), channel_id=1, source_target_pairs={{0,7},{1,0},{2,1},{3,2},{4,3},{5,4},{6,5},{7,6},{8,15},{9,8},{10,9... | collective-permute-start | bytes 6291464 | tf_op jit(solution)/shard_map/ppermute | solution.py:25
  305.9 4.8 copy-start.4
  305.9 6.2 %copy-start.6 = (bf16[2048,512]{1,0:T(8,128)(2,1)S(1)}, bf16[2048,512]{1,0:T(8,128)(2,1)}, u32[]{:S(2)}) copy-start(bf16[2048,512]{1,0:T(8,128)(2,1)} %copy-done.5) | copy-start | bytes 6291460
  305.9 7.7 %copy-start.8 = (bf16[2048,512]{1,0:T(8,128)(2,1)S(1)}, bf16[2048,512]{1,0:T(8,128)(2,1)}, u32[]{:S(2)}) copy-start(bf16[2048,512]{1,0:T(8,128)(2,1)} %copy-done.7) | copy-start | bytes 6291460
  309.1 6.0 %copy-start.10 = (bf16[2048,512]{1,0:T(8,128)(2,1)S(1)}, bf16[2048,512]{1,0:T(8,128)(2,1)}, u32[]{:S(2)}) copy-start(bf16[2048,512]{1,0:T(8,128)(2,1)} %copy-done.9) | copy-start | bytes 6291460
  313.6 35.0 %copy-start.2 = (bf16[2048,512]{1,0:T(8,128)(2,1)S(1)}, bf16[2048,512]{1,0:T(8,128)(2,1)}, u32[]{:S(2)}) copy-start(bf16[2048,512]{1,0:T(8,128)(2,1)} %param.11) | copy-start | bytes 6291460
  373.9 6.3 %copy-start.11 = (bf16[1,64,4096]{2,1,0:T(8,128)(2,1)S(1)}, bf16[1,64,4096]{2,1,0:T(8,128)(2,1)}, u32[]{:S(2)}) copy-start(bf16[1,64,4096]{2,1,0:T(8,128)(2,1)} %param.10) | copy-start | bytes 1572868
  373.9 6.8 %copy-start.13 = (bf16[4096]{0:T(1024)(128)(2,1)S(1)}, bf16[4096]{0:T(1024)(128)(2,1)}, u32[]{:S(2)}) copy-start(bf16[4096]{0:T(1024)(128)(2,1)} %param.12) | copy-start | bytes 24580
  379.6 53.2 %copy-start.12 = (bf16[1,128,512]{2,1,0:T(8,128)(2,1)S(1)}, bf16[1,128,512]{2,1,0:T(8,128)(2,1)}, u32[]{:S(2)}) copy-start(bf16[1,128,512]{2,1,0:T(8,128)(2,1)} %param.14) | copy-start | bytes 393220
  379.6 129.3 %all-gather.5.cloned.1.call-start = ((), (), s32[]{:S(2)}) async-start(), calls=%async_computation.3 | async-start | bytes 9437184 | tf_op jit(solution)/shard_map/all_gather | solution.py:40
  380.2 150.8 %all-gather.3.cloned.1.call-start = ((), (), s32[]{:S(2)}) async-start(), calls=%async_computation.2 | async-start | bytes 2621440 | tf_op jit(solution)/shard_map/all_gather | solution.py:37
  432.5 142.4 %reduce-scatter.5.cloned.1.call-start = ((), (), s32[]{:S(2)}) async-start(), calls=%async_computation.4 | async-start | bytes 2621440 | tf_op jit(solution)/shard_map/reduce_scatter | solution.py:67
  531.0 45.7 %copy-start.1 = (bf16[1,256,2048]{2,1,0:T(8,128)(2,1)S(1)}, bf16[1,256,2048]{2,1,0:T(8,128)(2,1)}, u32[]{:S(2)}) copy-start(bf16[1,256,2048]{2,1,0:T(8,128)(2,1)} %param.9) | copy-start | bytes 3145732
Sparse Core Ops, SparseCore 0:
  379.7 46.4 reduce-scatter.6
  543.4 31.4 reduce-scatter.4
Sparse Core Ops, SparseCore 1:
  382.4 126.4 all-gather.4
  510.3 20.6 all-gather.2
